TPU v7x, 256 devices: a whole 4x4x8 slice. The times are simulated.
256 devices in a mesh: pipe: 4 (over x), seq: 64 (over y, z, core).
Axes of the slice: x: 4, y: 4, z: 8, core: 2. Of those that a mesh axis runs over, the one named last changes fastest.
Arguments:
- inputs: bfloat16 [4, 8192, 2048], P('pipe', 'seq'), may hold values from -6 to 6
- lengths: int32 [4, 256], replicated, may hold values from 1 to 128, 8192 in all within a row
- order: int32 [4], replicated, may hold values from 0 to 3, each once
- norm_gain: float32 [4, 2048], P('pipe'), may hold values from 0.25 to 1.75
- rate: float32 [4, 16, 2048], P('pipe'), may hold values from 0.004 to 0.15
- angle: float32 [4, 16, 2048], P('pipe'), may hold values from -3.140625 to 3.140625
- coef: float32 [4, 2, 16, 2048], P('pipe'), may hold values from -0.3 to 0.3
- skip: float32 [4, 2048], P('pipe'), may hold values from 0.5 to 1.5
- score_gains: float32 [4, 2, 2048], P('pipe'), may hold values from -3 to 4.6
- out_proj: bfloat16 [4, 2048, 2048], P('pipe', 'seq'), may hold values from -0.125 to 0.125
Outputs:
- outputs: bfloat16 [4, 8192, 2048], P('pipe', 'seq')
Inputs may be any that keep to these rules, and one draw needn't show every extreme that they name: Each row of lengths sums to 8192, and every row holds a document of exactly 128 positions. `order`: each packed row appears once.
All inputs are finite; a program needn't handle non-finite values.
Results may differ from a plain program's by a relative error of at most 0.02.
The roundings to bfloat16 on the way count: a program that leaves them out, or rounds other values in their place, can miss the bound.
Values may be sent and summed in bfloat16 or wider, within the bound.
A program may use at most 128 MiB of HBM per device.

v0:
```python
import jax
import jax.numpy as jnp
from jax import lax
from jax.sharding import PartitionSpec as P

HEAD_DIM = 128


inner_span = 16
norm_eps = 1e-06
masked_score = -1e30


def passed_along(value, axis, steps):
    count = lax.axis_size(axis)
    initial, last = (max(0, -steps), min(count, count - steps))
    return lax.ppermute(value, axis, [(source, source + steps) for source in range(initial, last)])


def broadcast(value, axis, source):
    kept = jnp.where(lax.axis_index(axis) == source, value, 0).astype(value.dtype)
    return lax.psum(kept, axis)


def mode_powers(rate_now, angle_now, exponents):
    magnitude = jnp.exp(-exponents[:, None, None] * rate_now[None])
    turning = exponents[:, None, None] * angle_now[None]
    return (magnitude * jnp.cos(turning), magnitude * jnp.sin(turning))


def mode_tables(rate_now, angle_now, coef_now):
    lag_steps = jnp.arange(inner_span).astype(jnp.float32)
    coef_re = coef_now[0]
    coef_im = coef_now[1]
    power_re, power_im = mode_powers(rate_now, angle_now, lag_steps)
    kernel = 2.0 * jnp.sum(coef_re[None] * power_re - coef_im[None] * power_im, axis=1)
    ahead_re, ahead_im = mode_powers(rate_now, angle_now, lag_steps + 1.0)
    carry_re = coef_re[None] * ahead_re - coef_im[None] * ahead_im
    carry_im = coef_re[None] * ahead_im + coef_im[None] * ahead_re
    back_re, back_im = mode_powers(rate_now, angle_now, inner_span - 1.0 - lag_steps)
    whole_re, whole_im = mode_powers(
        rate_now, angle_now, jnp.full((1,), 1.0 * inner_span, jnp.float32)
    )
    return (kernel, carry_re, carry_im, back_re, back_im, whole_re[0], whole_im[0])


def local_conv(kernel, signal, doc_ids):
    result = kernel[0][None, None, :] * signal
    for lag_steps in range(1, inner_span):
        shifted = jnp.pad(signal[:, :-lag_steps], ((0, 0), (lag_steps, 0), (0, 0)))
        same_doc = jnp.pad(
            doc_ids[:, lag_steps:] == doc_ids[:, :-lag_steps], ((0, 0), (lag_steps, 0))
        )
        result = result + kernel[lag_steps][None, None, :] * shifted * same_doc[:, :, None].astype(
            jnp.float32
        )
    return result


def rms_scaled(values):
    return values * lax.rsqrt(jnp.mean(values * values, axis=1, keepdims=True) + norm_eps)


def block_terms(scaled, doc_ids, prior_first, tables_all, skip_now):
    kernel, carry_re, carry_im, back_re, back_im, whole_re, whole_im = tables_all
    block_count = scaled.shape[0] // inner_span
    blocks = scaled.reshape(block_count, inner_span, scaled.shape[1])
    block_docs = doc_ids.reshape(block_count, inner_span)
    last_docs = block_docs[:, -1]
    prior_docs = jnp.concatenate([jnp.reshape(prior_first, (1,)), last_docs[:-1]])
    base_out = local_conv(kernel, blocks, block_docs) + skip_now * blocks
    kept_rows = blocks * (block_docs == last_docs[:, None]).astype(jnp.float32)[:, :, None]
    local_re = jnp.sum(back_re[None] * kept_rows[:, :, None, :], axis=1)
    local_im = jnp.sum(back_im[None] * kept_rows[:, :, None, :], axis=1)
    link_flags = (last_docs == prior_docs).astype(jnp.float32)
    entry_flags = (block_docs == prior_docs[:, None]).astype(jnp.float32)
    return (base_out, local_re, local_im, link_flags, entry_flags)


def run_chain(local_re, local_im, link_flags, start_re, start_im, whole_re, whole_im):

    def advance(carried, item):
        state_re, state_im = carried
        piece_re, piece_im, link_now = item
        next_re = piece_re + link_now * (whole_re * state_re - whole_im * state_im)
        next_im = piece_im + link_now * (whole_re * state_im + whole_im * state_re)
        return ((next_re, next_im), (state_re, state_im))

    (end_re, end_im), (enter_re, enter_im) = lax.scan(
        advance, (start_re, start_im), (local_re, local_im, link_flags)
    )
    return (enter_re, enter_im, end_re, end_im)


def finish_terms(terms, tables_all, start_re, start_im):
    base_out, local_re, local_im, link_flags, entry_flags = terms
    carry_re = tables_all[1]
    carry_im = tables_all[2]
    enter_re, enter_im, end_re, end_im = run_chain(
        local_re, local_im, link_flags, start_re, start_im, tables_all[5], tables_all[6]
    )
    reached = 2.0 * jnp.sum(
        carry_re[None] * enter_re[:, None] - carry_im[None] * enter_im[:, None], axis=2
    )
    mixed = base_out + entry_flags[:, :, None] * reached
    return mixed.reshape(-1, mixed.shape[2])


def doc_attention(middle, key_rows, doc_ids, positions, gains_now, proj_whole):
    row_count = middle.shape[0]
    key_count = key_rows.shape[0]
    normed = rms_scaled(key_rows.astype(jnp.float32))
    query_heads = (
        (normed[key_count - row_count :] * gains_now[0])
        .astype(jnp.bfloat16)
        .reshape(row_count, -1, HEAD_DIM)
    )
    key_heads = (normed * gains_now[1]).astype(jnp.bfloat16).reshape(key_count, -1, HEAD_DIM)
    value_heads = key_rows.reshape(key_count, -1, HEAD_DIM)
    scores = jnp.einsum(
        "thd,shd->hts", query_heads, key_heads, preferred_element_type=jnp.float32
    ) * HEAD_DIM ** (-0.5)
    query_pos = positions[key_count - row_count :]
    query_docs = doc_ids[key_count - row_count :]
    allowed = (positions[None, :] <= query_pos[:, None]) & (doc_ids[None, :] == query_docs[:, None])
    scores = jnp.where(allowed[None], scores, masked_score)
    largest = jnp.max(scores, axis=2, keepdims=True)
    raw_weights = jnp.exp(scores - largest)
    weights = (raw_weights / jnp.sum(raw_weights, axis=2, keepdims=True)).astype(jnp.bfloat16)
    attended = jnp.einsum("hts,shd->thd", weights, value_heads, preferred_element_type=jnp.float32)
    attended = attended.reshape(row_count, -1).astype(jnp.bfloat16)
    projected = jnp.dot(attended, proj_whole, preferred_element_type=jnp.float32)
    return (middle.astype(jnp.float32) + projected).astype(jnp.bfloat16)


def section_layer(
    section_in, doc_ids, positions, tables_all, norm_now, skip_now, gains_now, proj_whole
):
    row_count = section_in.shape[0]
    zeros = jnp.zeros(tables_all[5].shape, jnp.float32)
    plain = section_in.astype(jnp.float32)
    scaled = rms_scaled(plain) * norm_now
    terms = block_terms(scaled, doc_ids[row_count:], doc_ids[row_count - 1], tables_all, skip_now)
    enter_re, enter_im, end_re, end_im = run_chain(
        terms[1], terms[2], terms[3], zeros, zeros, tables_all[5], tables_all[6]
    )
    arrived = passed_along(jnp.stack([end_re, end_im]), "seq", 1)
    mixed = finish_terms(terms, tables_all, arrived[0], arrived[1])
    middle = (plain + mixed).astype(jnp.bfloat16)
    before_middle = passed_along(middle, "seq", 1)
    key_rows = jnp.concatenate([before_middle, middle])
    return doc_attention(middle, key_rows, doc_ids, positions, gains_now, proj_whole)


def local(inputs, lengths, order, norm_gain, rate, angle, coef, skip, score_gains, out_proj):
    section_count = lax.axis_size("pipe")
    section_index = lax.axis_index("pipe")
    seq_index = lax.axis_index("seq")
    held_rows = inputs.shape[0]
    row_count = inputs.shape[1]
    width = inputs.shape[2]
    micro_count = section_count * held_rows
    tick_count = micro_count + section_count - 1
    whole_proj = lax.all_gather(out_proj[0], "seq", axis=0, tiled=True)
    tables_all = mode_tables(rate[0], angle[0], coef[0])
    positions = seq_index * row_count - row_count + jnp.arange(2 * row_count)
    silent_rows = jnp.zeros((row_count, width), jnp.bfloat16)
    incoming = silent_rows
    outgoing = silent_rows
    finished = []
    for moment in range(tick_count):
        if moment > 0:
            incoming = passed_along(outgoing, "pipe", 1)
        if moment < micro_count:
            entering = order[moment]
            local_row = lax.dynamic_index_in_dim(inputs, entering % held_rows, 0, False)
            fetched = broadcast(local_row, "pipe", entering // held_rows)
        else:
            fetched = silent_rows
        section_in = jnp.where(section_index == 0, fetched, incoming)
        slot_index = jnp.clip(moment - section_index, 0, micro_count - 1)
        chosen = lax.dynamic_index_in_dim(order, slot_index, 0, False)
        doc_ends = jnp.cumsum(lax.dynamic_index_in_dim(lengths, chosen, 0, False))
        counted = jnp.sum((doc_ends[None, :] <= positions[:, None]).astype(jnp.int32), axis=1)
        doc_ids = jnp.where(positions >= 0, counted, -1)
        outgoing = section_layer(
            section_in,
            doc_ids,
            positions,
            tables_all,
            norm_gain[0],
            skip[0],
            score_gains[0],
            whole_proj,
        )
        if moment >= section_count - 1:
            finished.append(outgoing)
    collected = jnp.stack(finished)
    handed = lax.all_to_all(collected, "pipe", split_axis=0, concat_axis=0, tiled=True)
    return handed[(section_count - 1) * held_rows : section_count * held_rows]


def solution(mesh):
    in_specs = (
        P("pipe", "seq", None),
        P(),
        P(),
        P("pipe", None),
        P("pipe", None, None),
        P("pipe", None, None),
        P("pipe", None, None, None),
        P("pipe", None),
        P("pipe", None, None),
        P("pipe", "seq", None),
    )
    out_specs = P("pipe", "seq", None)
    return jax.shard_map(local, mesh=mesh, in_specs=in_specs, out_specs=out_specs, check_vma=False)
```

profile of v0, /device:TPU:1, one launch (start us, length us, event | category | flops | bytes accessed | tf_op | source)
XLA Modules:
  0.0 1225.5 jit_solution(9369092443665512182)
XLA Ops:
  96.3 27.0 %multiply_subtract_fusion = (f32[16,16,2048]{2,1,0:T(8,128)S(1)}, f32[16,16,2048]{2,1,0:T(8,128)}, f32[16,2048]{1,0:T(8,128)S(1)}, f32[16,16,2048]{2,1,0:T(8,128)}, f32[16,16,2048]{2,1,0:T(8,128)}) fusion(f32[16]{0:T(128)} %get-tuple-element.1340, f32[16]{0:T(128)} %get-tuple-element.1342, f32[16,2048]{1,0:T(8,128)S(1)} %get-tuple-element.1271, ...), kind=kLoop, calls=%fused_computation.140 | loop fusion | flops 11501568 | bytes 9044352 | tf_op jit(solution)/shard_map/sub | solution.py:38
  176.2 29.5 %while.210 = (s32[]{:T(128)}, f32[16,2048]{1,0:T(8,128)S(1)}, f32[16,2048]{1,0:T(8,128)}, f32[8,16,2048]{2,1,0:T(8,128)}, f32[8]{0:T(128)}, /*index=5*/f32[16,20...) while((s32[]{:T(128)}, f32[16,2048]{1,0:T(8,128)S(1)}, ...), condition=%wide.region_12.13_spmd.clone, body=%wide.region_11.12_spmd.clone.sunk | while | flops 393219 | bytes 1048707 | solution.py:89
  225.0 42.2 %while.203 = (s32[]{:T(128)}, f32[16,2048]{1,0:T(8,128)}, f32[16,2048]{1,0:T(8,128)S(1)}, f32[8,16,2048]{2,1,0:T(8,128)}, f32[8,16,2048]{2,1,0:T(8,128)}, /*inde...) while((s32[]{:T(128)}, f32[16,2048]{1,0:T(8,128)}, ...), condition=%wide.region_14.15_spmd, body=%wide.region_13.14_spmd.sunk | while | flops 327682 | bytes 1573505 | solution.py:89
  267.5 7.6 subtract_reduce_fusion.6
  317.3 9.1 collective-permute-done.2
  332.8 28.5 %while.211 = (s32[]{:T(128)}, f32[16,2048]{1,0:T(8,128)S(1)}, f32[16,2048]{1,0:T(8,128)}, f32[8,16,2048]{2,1,0:T(8,128)}, f32[8]{0:T(128)}, /*index=5*/f32[16,20...) while((s32[]{:T(128)}, f32[16,2048]{1,0:T(8,128)S(1)}, ...), condition=%wide.region_26.27_spmd.clone, body=%wide.region_25.26_spmd.clone.sunk | while | flops 393219 | bytes 1048707 | solution.py:89
  380.5 42.8 %while.204 = (s32[]{:T(128)}, f32[16,2048]{1,0:T(8,128)}, f32[16,2048]{1,0:T(8,128)S(1)}, f32[8,16,2048]{2,1,0:T(8,128)}, f32[8,16,2048]{2,1,0:T(8,128)}, /*inde...) while((s32[]{:T(128)}, f32[16,2048]{1,0:T(8,128)}, ...), condition=%wide.region_28.29_spmd, body=%wide.region_27.28_spmd.sunk | while | flops 327682 | bytes 1573505 | solution.py:89
  423.6 7.7 subtract_reduce_fusion.5
  467.2 8.4 collective-permute-done.5
  482.1 29.6 %while.212 = (s32[]{:T(128)}, f32[16,2048]{1,0:T(8,128)S(1)}, f32[16,2048]{1,0:T(8,128)}, f32[8,16,2048]{2,1,0:T(8,128)}, f32[8]{0:T(128)}, /*index=5*/f32[16,20...) while((s32[]{:T(128)}, f32[16,2048]{1,0:T(8,128)S(1)}, ...), condition=%wide.region_40.41_spmd.clone, body=%wide.region_39.40_spmd.clone.sunk | while | flops 393219 | bytes 1048707 | solution.py:89
  513.3 6.2 collective-permute-start.6
  532.4 42.6 %while.205 = (s32[]{:T(128)}, f32[16,2048]{1,0:T(8,128)}, f32[16,2048]{1,0:T(8,128)S(1)}, f32[8,16,2048]{2,1,0:T(8,128)}, f32[8,16,2048]{2,1,0:T(8,128)}, /*inde...) while((s32[]{:T(128)}, f32[16,2048]{1,0:T(8,128)}, ...), condition=%wide.region_42.43_spmd, body=%wide.region_41.42_spmd.sunk | while | flops 327682 | bytes 1573505 | solution.py:89
  575.3 7.7 subtract_reduce_fusion.4
  619.0 8.3 collective-permute-done.8
  633.7 28.0 %while.213 = (s32[]{:T(128)}, f32[16,2048]{1,0:T(8,128)S(1)}, f32[16,2048]{1,0:T(8,128)}, f32[8,16,2048]{2,1,0:T(8,128)}, f32[8]{0:T(128)}, /*index=5*/f32[16,20...) while((s32[]{:T(128)}, f32[16,2048]{1,0:T(8,128)S(1)}, ...), condition=%wide.region_54.55_spmd.clone, body=%wide.region_53.54_spmd.clone.sunk | while | flops 393219 | bytes 1048707 | solution.py:89
  663.3 7.2 collective-permute-start.9
  683.4 40.9 %while.206 = (s32[]{:T(128)}, f32[16,2048]{1,0:T(8,128)}, f32[16,2048]{1,0:T(8,128)S(1)}, f32[8,16,2048]{2,1,0:T(8,128)}, f32[8,16,2048]{2,1,0:T(8,128)}, /*inde...) while((s32[]{:T(128)}, f32[16,2048]{1,0:T(8,128)}, ...), condition=%wide.region_56.57_spmd, body=%wide.region_55.56_spmd.sunk | while | flops 327682 | bytes 1573505 | solution.py:89
  724.7 7.7 subtract_reduce_fusion.3
  768.2 8.4 collective-permute-done.11
  781.7 28.7 %while.214 = (s32[]{:T(128)}, f32[16,2048]{1,0:T(8,128)S(1)}, f32[16,2048]{1,0:T(8,128)}, f32[8,16,2048]{2,1,0:T(8,128)}, f32[8]{0:T(128)}, /*index=5*/f32[16,20...) while((s32[]{:T(128)}, f32[16,2048]{1,0:T(8,128)S(1)}, ...), condition=%wide.region_68.69_spmd.clone, body=%wide.region_67.68_spmd.clone.sunk | while | flops 393219 | bytes 1048707 | solution.py:89
  830.0 41.7 %while.207 = (s32[]{:T(128)}, f32[16,2048]{1,0:T(8,128)}, f32[16,2048]{1,0:T(8,128)S(1)}, f32[8,16,2048]{2,1,0:T(8,128)}, f32[8,16,2048]{2,1,0:T(8,128)}, /*inde...) while((s32[]{:T(128)}, f32[16,2048]{1,0:T(8,128)}, ...), condition=%wide.region_70.71_spmd, body=%wide.region_69.70_spmd.sunk | while | flops 327682 | bytes 1573505 | solution.py:89
  872.0 7.7 subtract_reduce_fusion.2
  915.6 8.7 collective-permute-done.14
  929.4 29.0 %while.215 = (s32[]{:T(128)}, f32[16,2048]{1,0:T(8,128)S(1)}, f32[16,2048]{1,0:T(8,128)}, f32[8,16,2048]{2,1,0:T(8,128)}, f32[8]{0:T(128)}, /*index=5*/f32[16,20...) while((s32[]{:T(128)}, f32[16,2048]{1,0:T(8,128)S(1)}, ...), condition=%wide.region_82.83_spmd.clone, body=%wide.region_81.82_spmd.clone.sunk | while | flops 393219 | bytes 1048707 | solution.py:89
  977.5 36.8 %while.208 = (s32[]{:T(128)}, f32[16,2048]{1,0:T(8,128)}, f32[16,2048]{1,0:T(8,128)S(1)}, f32[8,16,2048]{2,1,0:T(8,128)}, f32[8,16,2048]{2,1,0:T(8,128)}, /*inde...) while((s32[]{:T(128)}, f32[16,2048]{1,0:T(8,128)}, ...), condition=%wide.region_84.85_spmd, body=%wide.region_83.84_spmd.sunk | while | flops 327682 | bytes 1573505 | solution.py:89
  1014.6 7.7 subtract_reduce_fusion.1
  1058.2 8.3 collective-permute-done.17
  1071.7 28.4 %while.216 = (s32[]{:T(128)}, f32[16,2048]{1,0:T(8,128)S(1)}, f32[16,2048]{1,0:T(8,128)}, f32[8,16,2048]{2,1,0:T(8,128)}, f32[8]{0:T(128)}, /*index=5*/f32[16,20...) while((s32[]{:T(128)}, f32[16,2048]{1,0:T(8,128)S(1)}, ...), condition=%wide.region_96.97_spmd.clone, body=%wide.region_95.96_spmd.clone.sunk | while | flops 393219 | bytes 1048707 | solution.py:89
  1101.0 5.2 collective-permute-start.18
  1117.8 36.9 %while.209 = (s32[]{:T(128)}, f32[16,2048]{1,0:T(8,128)}, f32[16,2048]{1,0:T(8,128)S(1)}, f32[8,16,2048]{2,1,0:T(8,128)}, f32[8,16,2048]{2,1,0:T(8,128)}, /*inde...) while((s32[]{:T(128)}, f32[16,2048]{1,0:T(8,128)}, ...), condition=%wide.region_98.99_spmd, body=%wide.region_97.98_spmd.sunk | while | flops 327682 | bytes 1573505 | solution.py:89
  1155.1 7.7 subtract_reduce_fusion
  1188.9 28.1 %all_to_all.5 = bf16[4,128,2048]{2,1,0:T(8,128)(2,1)S(1)} all-to-all(bf16[4,128,2048]{2,1,0:T(8,128)(2,1)S(1)} %pad_maximum_fusion), channel_id=1, replica_groups=mesh['pipe'=4,'seq'=64] {'pipe'}, dimensions={0} | all-to-all | bytes 4194304 | tf_op jit(solution)/shard_map/all_to_all | solution.py:199
  (1637 shorter events, 1009.9 us)
Async XLA Ops:
  7.4 161.3 %all-reduce.213.cloned.1.call-start = ((), (), s32[]{:S(2)}) async-start(), calls=%async_computation.2 | async-start | bytes 4194304 | tf_op jit(solution)/shard_map/psum | solution.py:22
  14.1 294.8 %all-gather.3.cloned.1.call-start = ((), (), s32[]{:S(2)}) async-start(), calls=%async_computation.1 | async-start | bytes 8519680 | tf_op jit(solution)/shard_map/all_gather | solution.py:164
  32.5 90.8 %copy-start.31 = (s32[16,16]{1,0:T(8,128)}, s32[16,16]{1,0:T(8,128)S(1)}, u32[]{:S(2)}) copy-start(s32[16,16]{1,0:T(8,128)S(1)} %broadcast_select_fusion.11) | copy-start | bytes 3076
  32.7 128.9 %copy-start.340 = (s32[8]{0:T(128)}, s32[8]{0:T(128)S(1)}, u32[]{:S(2)}) copy-start(s32[8]{0:T(128)S(1)} %slice_reduce_fusion.11) | copy-start | bytes 100
  33.5 89.8 %copy-start.33 = (s32[16,16]{1,0:T(8,128)}, s32[16,16]{1,0:T(8,128)S(1)}, u32[]{:S(2)}) copy-start(s32[16,16]{1,0:T(8,128)S(1)} %broadcast_select_fusion.12) | copy-start | bytes 3076
  33.6 127.9 %copy-start.342 = (s32[8]{0:T(128)}, s32[8]{0:T(128)S(1)}, u32[]{:S(2)}) copy-start(s32[8]{0:T(128)S(1)} %slice_reduce_fusion.12) | copy-start | bytes 100
  34.4 88.9 %copy-start.344 = (s32[256]{0:T(256)}, s32[256]{0:T(256)S(1)}, u32[]{:S(2)}) copy-start(s32[256]{0:T(256)S(1)} %broadcast_select_fusion.19) | copy-start | bytes 3076
  34.4 88.9 %copy-start.345 = (s32[256]{0:T(256)}, s32[256]{0:T(256)S(1)}, u32[]{:S(2)}) copy-start(s32[256]{0:T(256)S(1)} %broadcast_select_fusion.18) | copy-start | bytes 3076
  34.5 88.8 %copy-start.35 = (s32[16,16]{1,0:T(8,128)}, s32[16,16]{1,0:T(8,128)S(1)}, u32[]{:S(2)}) copy-start(s32[16,16]{1,0:T(8,128)S(1)} %broadcast_select_fusion.13) | copy-start | bytes 3076
  35.5 87.8 %copy-start.346 = (s32[256]{0:T(256)}, s32[256]{0:T(256)S(1)}, u32[]{:S(2)}) copy-start(s32[256]{0:T(256)S(1)} %broadcast_select_fusion.20) | copy-start | bytes 3076
  66.6 97.5 %copy-start.338 = (s32[8]{0:T(128)}, s32[8]{0:T(128)S(1)}, u32[]{:S(2)}) copy-start(s32[8]{0:T(128)S(1)} %slice_reduce_fusion.10) | copy-start | bytes 100
  68.3 95.8 %copy-start.336 = (s32[8]{0:T(128)}, s32[8]{0:T(128)S(1)}, u32[]{:S(2)}) copy-start(s32[8]{0:T(128)S(1)} %slice_reduce_fusion.9) | copy-start | bytes 100
  207.4 13.7 %collective-permute-start = (f32[2,16,2048]{2,1,0:T(8,128)}, f32[2,16,2048]{2,1,0:T(8,128)}, u32[]{:S(2)}, u32[]{:S(2)}) collective-permute-start(f32[2,16,2048]{2,1,0:T(8,128)} %pad_maximum_fusion.8), channel_id=1, source_target_pairs={{0,1},{1,2},{2,3},{3,4},{4,5},{5,6},{6,7},{7,8},{8,9},{9,10},{10,1... | collective-permute-start | bytes 786440 | tf_op jit(solution)/shard_map/ppermute | solution.py:17
  279.7 15.3 %collective-permute-start.1 = (bf16[128,2048]{1,0:T(8,128)(2,1)S(1)}, bf16[128,2048]{1,0:T(8,128)(2,1)S(1)}, u32[]{:S(2)}, u32[]{:S(2)}) collective-permute-start(bf16[128,2048]{1,0:T(8,128)(2,1)S(1)} %fusion.46), channel_id=1, source_target_pairs={{0,1},{1,2},{2,3},{3,4},{4,5},{5,6},{6,7},{7,8},{8,9},{9,10},{10,1... | collective-permute-start | bytes 1572872 | tf_op jit(solution)/shard_map/ppermute | solution.py:17
  313.8 12.6 %collective-permute-start.2 = (bf16[128,2048]{1,0:T(8,128)(2,1)S(1)}, bf16[128,2048]{1,0:T(8,128)(2,1)S(1)}, u32[]{:S(2)}, u32[]{:S(2)}) collective-permute-start(bf16[128,2048]{1,0:T(8,128)(2,1)S(1)} %fusion.24), channel_id=1, source_target_pairs={{0,64},{64,128},{128,192},{1,65},{65,129},{129,193},{2,66},{66,130... | collective-permute-start | bytes 1572872 | tf_op jit(solution)/shard_map/ppermute | solution.py:17
  363.0 13.6 %collective-permute-start.3 = (f32[2,16,2048]{2,1,0:T(8,128)}, f32[2,16,2048]{2,1,0:T(8,128)}, u32[]{:S(2)}, u32[]{:S(2)}) collective-permute-start(f32[2,16,2048]{2,1,0:T(8,128)} %pad_maximum_fusion.9), channel_id=1, source_target_pairs={{0,1},{1,2},{2,3},{3,4},{4,5},{5,6},{6,7},{7,8},{8,9},{9,10},{10,1... | collective-permute-start | bytes 786440 | tf_op jit(solution)/shard_map/ppermute | solution.py:17
  435.8 8.0 collective-permute-start.4
  461.7 13.9 %collective-permute-start.5 = (bf16[128,2048]{1,0:T(8,128)(2,1)S(1)}, bf16[128,2048]{1,0:T(8,128)(2,1)S(1)}, u32[]{:S(2)}, u32[]{:S(2)}) collective-permute-start(bf16[128,2048]{1,0:T(8,128)(2,1)S(1)} %add_convert_fusion.5), channel_id=1, source_target_pairs={{0,64},{64,128},{128,192},{1,65},{65,129},{129,193},{2,66},{66,130... | collective-permute-start | bytes 1572872 | tf_op jit(solution)/shard_map/ppermute | solution.py:17
  513.3 15.1 %collective-permute-start.6 = (f32[2,16,2048]{2,1,0:T(8,128)}, f32[2,16,2048]{2,1,0:T(8,128)}, u32[]{:S(2)}, u32[]{:S(2)}) collective-permute-start(f32[2,16,2048]{2,1,0:T(8,128)} %pad_maximum_fusion.10), channel_id=1, source_target_pairs={{0,1},{1,2},{2,3},{3,4},{4,5},{5,6},{6,7},{7,8},{8,9},{9,10},{10,1... | collective-permute-start | bytes 786440 | tf_op jit(solution)/shard_map/ppermute | solution.py:17
  587.5 8.0 collective-permute-start.7
  613.4 13.8 %collective-permute-start.8 = (bf16[128,2048]{1,0:T(8,128)(2,1)S(1)}, bf16[128,2048]{1,0:T(8,128)(2,1)S(1)}, u32[]{:S(2)}, u32[]{:S(2)}) collective-permute-start(bf16[128,2048]{1,0:T(8,128)(2,1)S(1)} %add_convert_fusion.4), channel_id=1, source_target_pairs={{0,64},{64,128},{128,192},{1,65},{65,129},{129,193},{2,66},{66,130... | collective-permute-start | bytes 1572872 | tf_op jit(solution)/shard_map/ppermute | solution.py:17
  663.3 16.2 %collective-permute-start.9 = (f32[2,16,2048]{2,1,0:T(8,128)}, f32[2,16,2048]{2,1,0:T(8,128)}, u32[]{:S(2)}, u32[]{:S(2)}) collective-permute-start(f32[2,16,2048]{2,1,0:T(8,128)} %pad_maximum_fusion.11), channel_id=1, source_target_pairs={{0,1},{1,2},{2,3},{3,4},{4,5},{5,6},{6,7},{7,8},{8,9},{9,10},{10,1... | collective-permute-start | bytes 786440 | tf_op jit(solution)/shard_map/ppermute | solution.py:17
  736.9 8.0 collective-permute-start.10
  762.6 13.9 %collective-permute-start.11 = (bf16[128,2048]{1,0:T(8,128)(2,1)S(1)}, bf16[128,2048]{1,0:T(8,128)(2,1)S(1)}, u32[]{:S(2)}, u32[]{:S(2)}) collective-permute-start(bf16[128,2048]{1,0:T(8,128)(2,1)S(1)} %add_convert_fusion.3), channel_id=1, source_target_pairs={{0,64},{64,128},{128,192},{1,65},{65,129},{129,193},{2,66},{66,130... | collective-permute-start | bytes 1572872 | tf_op jit(solution)/shard_map/ppermute | solution.py:17
  812.1 14.0 %collective-permute-start.12 = (f32[2,16,2048]{2,1,0:T(8,128)}, f32[2,16,2048]{2,1,0:T(8,128)}, u32[]{:S(2)}, u32[]{:S(2)}) collective-permute-start(f32[2,16,2048]{2,1,0:T(8,128)} %pad_maximum_fusion.12), channel_id=1, source_target_pairs={{0,1},{1,2},{2,3},{3,4},{4,5},{5,6},{6,7},{7,8},{8,9},{9,10},{10,1... | collective-permute-start | bytes 786440 | tf_op jit(solution)/shard_map/ppermute | solution.py:17
  884.2 8.0 collective-permute-start.13
  910.0 14.2 %collective-permute-start.14 = (bf16[128,2048]{1,0:T(8,128)(2,1)S(1)}, bf16[128,2048]{1,0:T(8,128)(2,1)S(1)}, u32[]{:S(2)}, u32[]{:S(2)}) collective-permute-start(bf16[128,2048]{1,0:T(8,128)(2,1)S(1)} %add_convert_fusion.2), channel_id=1, source_target_pairs={{0,64},{64,128},{128,192},{1,65},{65,129},{129,193},{2,66},{66,130... | collective-permute-start | bytes 1572872 | tf_op jit(solution)/shard_map/ppermute | solution.py:17
  960.1 13.5 %collective-permute-start.15 = (f32[2,16,2048]{2,1,0:T(8,128)}, f32[2,16,2048]{2,1,0:T(8,128)}, u32[]{:S(2)}, u32[]{:S(2)}) collective-permute-start(f32[2,16,2048]{2,1,0:T(8,128)} %pad_maximum_fusion.13), channel_id=1, source_target_pairs={{0,1},{1,2},{2,3},{3,4},{4,5},{5,6},{6,7},{7,8},{8,9},{9,10},{10,1... | collective-permute-start | bytes 786440 | tf_op jit(solution)/shard_map/ppermute | solution.py:17
  1026.8 8.0 collective-permute-start.16
  1052.6 13.9 %collective-permute-start.17 = (bf16[128,2048]{1,0:T(8,128)(2,1)S(1)}, bf16[128,2048]{1,0:T(8,128)(2,1)S(1)}, u32[]{:S(2)}, u32[]{:S(2)}) collective-permute-start(bf16[128,2048]{1,0:T(8,128)(2,1)S(1)} %add_convert_fusion.1), channel_id=1, source_target_pairs={{0,64},{64,128},{128,192},{1,65},{65,129},{129,193},{2,66},{66,130... | collective-permute-start | bytes 1572872 | tf_op jit(solution)/shard_map/ppermute | solution.py:17
  1101.0 14.0 %collective-permute-start.18 = (f32[2,16,2048]{2,1,0:T(8,128)S(1)}, f32[2,16,2048]{2,1,0:T(8,128)S(1)}, u32[]{:S(2)}, u32[]{:S(2)}) collective-permute-start(f32[2,16,2048]{2,1,0:T(8,128)S(1)} %pad_maximum_fusion.14), channel_id=1, source_target_pairs={{0,1},{1,2},{2,3},{3,4},{4,5},{5,6},{6,7},{7,8},{8,9},{9,10},{10,1... | collective-permute-start | bytes 786440 | tf_op jit(solution)/shard_map/ppermute | solution.py:17
  1167.2 8.0 collective-permute-start.19
  (401 other events, 5646.4 us)
Sparse Core Ops, SparseCore 0:
  14.2 68.0 all-reduce.212
Sparse Core Ops, SparseCore 1:
  17.7 87.8 all-gather.2
where the time goes:
time: 1240 us; the launch traced here: 1230 us
  other arithmetic  580 us (47%)
  local copies, waits for them, and re-layouts  354 us (29%)
  matrix products  78.5 us (6%)
  starting transfers between devices  76.1 us (6%)
  waiting for transfers between devices  70.9 us (6%)
  between operations  36.8 us (3%)
  blocking collectives  28.1 us (2%)
    add x112, other arithmetic, advance(): next_im = piece_im + link_now * (whole_re * state_im + whole_im * state_re)  267 us
    dynamic_slice x112, local copies, waits for them, and re-layouts, run_chain(): lax.scan(advance, (start_re, start_im), (local_re, local_im, link_flags))  127 us
    dynamic_update_slice x56, local copies, waits for them, and re-layouts, run_chain(): lax.scan(advance, (start_re, start_im), (local_re, local_im, link_flags))  90.9 us
    ppermute x20, starting transfers between devices, passed_along(): lax.ppermute(value, axis, [(source, source + steps) for source in range(i...  76.1 us
    ppermute x20, waiting for transfers between devices, passed_along(): lax.ppermute(value, axis, [(source, source + steps) for source in range(i...  70.4 us
    eq x105, other arithmetic, local_conv(): doc_ids[:, lag_steps:] == doc_ids[:, :-lag_steps]  59.2 us
    reduce_sum x7, other arithmetic, finish_terms(): jnp.sum(carry_re[None] * enter_re[:, None] - carry_im[None] * enter_im[:,...  53.8 us
    convert_element_type x56, other arithmetic, local_conv(): same_doc[:, :, None].astype(jnp.float32)  53.5 us
  transfers between devices with their start and end apart: 22, of which 12 were waited for; matrix products, arithmetic and copies ran while one was open for 28% of the time, Pallas kernels for 0%

commit v1 on v0

v1 whole, which is shorter than its diff:
```python
import functools

import jax
import jax.numpy as jnp
from jax import lax
from jax.experimental import pallas as pl
from jax.experimental.pallas import tpu as pltpu
from jax.sharding import PartitionSpec as P

HEAD_DIM = 128
LANES = 128
norm_eps = 1e-06
masked_score = -1e30


MESH = pl.DeviceIdType.MESH
ZS, YS, XS = 8, 4, 4


class Mover:
    def __init__(self, send_sems, recv_sems):
        self.send_sems, self.recv_sems, self.used, self.open = send_sems, recv_sems, 0, []

    def push(self, source, target, incoming, device):
        k = self.used
        self.used += 1
        out = pltpu.make_async_remote_copy(source, target, self.send_sems.at[k], self.recv_sems.at[k],
                                           device_id=device, device_id_type=MESH)
        out.start()
        back = pltpu.make_async_remote_copy(incoming, incoming, self.send_sems.at[k], self.recv_sems.at[k],
                                            device_id=device, device_id_type=MESH)
        self.open.append(out)
        return back.wait_recv

    def finish(self):
        for out in self.open:
            out.wait_send()
        self.open = []


def ring(mover, size, me, block, half, device):
    def at(shift):
        return lax.rem(me + (shift + size), size)
    waits = {}

    def step(t):
        def go():
            if t > 1:
                waits[t - 1, 0]()
                waits[t - 1, 1]()
            if t <= size // 2:
                pick = (lambda i, k: half(i, k)) if t == size // 2 else (lambda i, k: block(i))
                ahead, behind = at(1 - t), at(t - 1)
                waits[t, 0] = mover.push(pick(ahead, 0), pick(ahead, 0), pick(at(-t), 0), device(at(1)))
                waits[t, 1] = mover.push(pick(behind, 1), pick(behind, 1), pick(at(t), 1), device(at(-1)))
        return go
    return [step(t) for t in range(1, size // 2 + 2)]


def transfer_steps(mover, refs, chosen, width, split):
    w_ref, in_ref, tab_in, wg, xin, tabs, x, local_sem = refs
    pipe, seq = lax.axis_index("pipe"), lax.axis_index("seq")
    core, z, y = lax.rem(seq, 2), lax.rem(seq // 2, ZS), seq // (2 * ZS)
    rows = in_ref.shape[0]
    nseq = 2 * ZS * YS

    def seq_of(yy, zz, cc):
        return (yy * ZS + zz) * 2 + cc

    def to_x(i):
        return (i, seq)

    def to_y(i):
        return (pipe, seq_of(i, z, core))

    def to_z(i):
        return (pipe, seq_of(y, i, core))

    partner = (pipe, seq_of(y, z, 1 - core))
    following = (pipe, lax.rem(seq + 1, nseq))
    preceding = (pipe, lax.rem(seq + nseq - 1, nseq))
    peers = [to_x(lax.rem(pipe + 1, XS)), to_x(lax.rem(pipe + 3, XS)), to_y(lax.rem(y + 1, YS)), to_y(lax.rem(y + 3, YS)),
             to_z(lax.rem(z + 1, ZS)), to_z(lax.rem(z + 7, ZS)), partner, following, preceding]
    trows = tabs.shape[1] // 2
    tlow = pl.ds(core * trows, trows)
    tpart = [pl.ds(core * trows + k * (trows // 2), trows // 2) for k in range(2)]
    depth = w_ref.shape[0]

    def begin():
        bar = pltpu.get_barrier_semaphore()
        for peer in peers:
            pl.semaphore_signal(bar, inc=1, device_id=peer, device_id_type=MESH)
        pl.semaphore_wait(bar, len(peers))
        copies = [pltpu.make_async_copy(w_ref, wg.at[pipe, y, z, core], local_sem.at[0]),
                  pltpu.make_async_copy(in_ref, xin.at[pipe], local_sem.at[1]),
                  pltpu.make_async_copy(tab_in.at[tlow], tabs.at[pipe, tlow], local_sem.at[2])]
        for c in copies:
            c.start()
        for c in copies:
            c.wait()

    xw = ring(mover, XS, pipe, lambda i: wg.at[i, y, z, core],
              lambda i, k: wg.at[i, y, z, core, pl.ds(k * (depth // 2), depth // 2)], to_x)
    xi = ring(mover, XS, pipe, lambda i: xin.at[i], lambda i, k: xin.at[i, pl.ds(k * (rows // 2), rows // 2)], to_x)
    xt = ring(mover, XS, pipe, lambda i: tabs.at[i, tlow], lambda i, k: tabs.at[i, tpart[k]], to_x)
    ca, cb = pl.ds(0, split), pl.ds(split, width - split)
    pair = [pl.ds(0, XS // 2), pl.ds(XS // 2, XS // 2)]
    ya = ring(mover, YS, y, lambda i: wg.at[:, i, z, core, :, ca], lambda i, k: wg.at[pair[k], i, z, core, :, ca], to_y)
    zb = ring(mover, ZS, z, lambda i: wg.at[:, y, i, core, :, cb], lambda i, k: wg.at[pair[k], y, i, core, :, cb], to_z)
    held = {}

    def choose():
        x[pl.ds(rows, rows), :] = xin[chosen]
        held["halo"] = mover.push(x.at[pl.ds(rows, rows)], x.at[pl.ds(0, rows)], x.at[pl.ds(0, rows)], following)

    def share_tables():
        other = pl.ds((1 - core) * trows, trows)
        held["tabs"] = mover.push(tabs.at[:, tlow], tabs.at[:, tlow], tabs.at[:, other], partner)

    def last(s):
        yh = [pl.ds(0, YS // 2), pl.ds(YS // 2, YS // 2)]
        zh = [pl.ds(0, ZS // 2), pl.ds(ZS // 2, ZS // 2)]
        za = ring(mover, ZS, z, lambda i: wg.at[s, :, i, core, :, ca], lambda i, k: wg.at[s, yh[k], i, core, :, ca], to_z)
        yb = ring(mover, YS, y, lambda i: wg.at[s, i, :, core, :, cb], lambda i, k: wg.at[s, i, zh[k], core, :, cb], to_y)
        return za, yb

    def swap(s):
        held["w", s] = mover.push(wg.at[s, :, :, core], wg.at[s, :, :, core], wg.at[s, :, :, 1 - core], partner)

    finals = [last(s) for s in range(XS)]
    early = [begin, xw[0], xw[1], xi[0], xw[2], ya[0], zb[0], xt[0], zb[1], ya[1], xi[1], zb[2], ya[2], zb[3], xt[1], xi[2], choose,
             xt[2], share_tables, zb[4]]
    wait_inputs = [lambda: held["halo"](), lambda: held["tabs"]()]
    per_section = []
    for s in range(XS):
        za, yb = finals[s]
        steps = [] if s else [za[0], yb[0]]
        steps += [za[1], za[2], yb[1], za[3]]
        if s + 1 < XS:
            steps += [finals[s + 1][0][0], finals[s + 1][1][0]]
        steps += [za[4], yb[2], functools.partial(swap, s)]
        per_section.append((steps, (lambda s=s: held["w", s]())))
    return early, wait_inputs, per_section


def comm_kernel(width, split, order_ref, w_ref, in_ref, tab_in, wg, tabs, x, xin, send_sems, recv_sems, local_sem):
    mover = Mover(send_sems, recv_sems)
    chosen = order_ref[lax.axis_index("pipe")]
    early, wait_inputs, per_section = transfer_steps(
        mover, (w_ref, in_ref, tab_in, wg, xin, tabs, x, local_sem), chosen, width, split)
    for step in early + wait_inputs:
        step()
    for steps, done in per_section:
        for step in steps:
            step()
    for steps, done in per_section:
        done()
    mover.finish()


def compute_kernel(sections, modes, rows, width, x_ref, link_ref, docq_ref, dock_ref, tab_ref, w_hbm, o_ref,
                   cur, xs, ys, mid, qs, ks, att, bias, wbuf, wsem):
    groups = width // LANES
    halves = groups // 8
    own = rows // 2
    f32, bf16 = jnp.float32, jnp.bfloat16

    def fetch(s, slot):
        return pltpu.make_async_copy(w_hbm.at[s], wbuf.at[slot], wsem.at[slot])

    fetch(0, 0).start()
    cur[...] = x_ref[...]
    qpos = lax.broadcasted_iota(jnp.int32, (own, rows), 0) + own
    kpos = lax.broadcasted_iota(jnp.int32, (own, rows), 1)
    for half in range(2):
        good = (docq_ref[half * own:(half + 1) * own, :] == dock_ref[...]) & (kpos <= qpos - (1 - half) * own)
        bias[half * own:(half + 1) * own, :] = jnp.where(good, 0.0, masked_score)

    def section(s, carry):
        slot = s % 2

        @pl.when(s + 1 < sections)
        def _():
            fetch(s + 1, 1 - slot).start()

        def spread(r, c):
            base = pl.multiple_of(r * 16, 16)
            xb = cur[pl.ds(base, 16), :].astype(f32)
            inv = lax.rsqrt(jnp.mean(xb * xb, axis=1, keepdims=True) + norm_eps)
            for g in range(groups):
                sc = xb[:, g * LANES:(g + 1) * LANES] * inv * tab_ref[s, 4 * modes, g:g + 1, :]
                for h in range(2):
                    xs[pl.ds((base + 8 * h) * groups + g, 8, stride=groups), :] = sc[8 * h:8 * h + 8]
            return c

        lax.fori_loop(0, rows // 16, spread, 0)

        per = 8
        for hf in range(halves):
            for mg in range(modes // per):
                c1 = [tab_ref[s, mg * per + m, 8 * hf:8 * hf + 8, :] for m in range(per)]
                c2 = [tab_ref[s, modes + mg * per + m, 8 * hf:8 * hf + 8, :] for m in range(per)]
                b0 = [tab_ref[s, 2 * modes + mg * per + m, 8 * hf:8 * hf + 8, :] for m in range(per)]
                b1 = [tab_ref[s, 3 * modes + mg * per + m, 8 * hf:8 * hf + 8, :] for m in range(per)]
                skip = tab_ref[s, 4 * modes + 1, 8 * hf:8 * hf + 8, :]

                def step(p0, state, c1=c1, c2=c2, b0=b0, b1=b1, skip=skip, hf=hf, mg=mg):
                    w1, w2 = list(state[:per]), list(state[per:])
                    for u in range(4):
                        p = p0 * 4 + u
                        at = pl.multiple_of(p * groups + 8 * hf, 8)
                        x = xs[pl.ds(at, 8), :]
                        link = link_ref[0, p]
                        acc = skip * x if mg == 0 else ys[pl.ds(at, 8), :]
                        parts = []
                        for m in range(per):
                            k1 = w1[m] * link
                            k2 = w2[m] * link
                            w = x + (c1[m] * k1 + c2[m] * k2)
                            parts.append(b0[m] * w + b1[m] * k1)
                            w1[m], w2[m] = w, k1
                        while len(parts) > 1:
                            parts = [parts[i] + parts[i + 1] for i in range(0, len(parts), 2)]
                        ys[pl.ds(at, 8), :] = acc + parts[0]
                    return tuple(w1) + tuple(w2)

                zero = jnp.zeros((8, LANES), f32)
                lax.fori_loop(0, rows // 4, step, (zero,) * (2 * per))

        def gather(r, c):
            base = pl.multiple_of(r * 16, 16)
            sq = jnp.zeros((16, LANES), f32)
            mids = []
            for g in range(groups):
                mixed = jnp.concatenate(
                    [ys[pl.ds((base + 8 * h) * groups + g, 8, stride=groups), :] for h in range(2)], axis=0)
                mb = (cur[pl.ds(base, 16), g * LANES:(g + 1) * LANES].astype(f32) + mixed).astype(bf16)
                mid[pl.ds(base, 16), g * LANES:(g + 1) * LANES] = mb
                mf = mb.astype(f32)
                sq = sq + mf * mf
            inv = lax.rsqrt(jnp.sum(sq, axis=1, keepdims=True) * (1.0 / width) + norm_eps)
            for g in range(groups):
                lanes = slice(g * LANES, (g + 1) * LANES)
                normed = mid[pl.ds(base, 16), lanes].astype(f32) * inv
                qs[pl.ds(base, 16), lanes] = (normed * tab_ref[s, 4 * modes + 2, g:g + 1, :]).astype(bf16)
                ks[pl.ds(base, 16), lanes] = (normed * tab_ref[s, 4 * modes + 3, g:g + 1, :]).astype(bf16)
            return c

        lax.fori_loop(0, rows // 16, gather, 0)

        def head(h, c):
            lanes = pl.ds(pl.multiple_of(h * HEAD_DIM, HEAD_DIM), HEAD_DIM)
            for half in range(2):
                qrows = slice(half * own, (half + 1) * own)
                krows = slice(0, (half + 1) * own)
                scores = lax.dot_general(qs[qrows, lanes], ks[krows, lanes], (((1,), (1,)), ((), ())),
                                         preferred_element_type=f32) * HEAD_DIM ** (-0.5)
                scores = scores + bias[qrows, krows]
                largest = jnp.max(scores, axis=1, keepdims=True)
                raw = jnp.exp(scores - largest)
                weights = (raw / jnp.sum(raw, axis=1, keepdims=True)).astype(bf16)
                att[qrows, lanes] = jnp.dot(weights, mid[krows, lanes], preferred_element_type=f32).astype(bf16)
            return c

        lax.fori_loop(0, width // HEAD_DIM, head, 0)

        fetch(s, slot).wait()
        cols = 256

        def project(n, c):
            lanes = pl.ds(pl.multiple_of(n * cols, cols), cols)
            acc = jnp.dot(att[...], wbuf[slot, :, lanes], preferred_element_type=f32)
            cur[:, lanes] = (mid[:, lanes].astype(f32) + acc).astype(bf16)
            return c

        lax.fori_loop(0, width // cols, project, 0)
        return carry

    lax.fori_loop(0, sections, section, 0)
    o_ref[...] = cur[own:, :]


def mode_table(rate, angle, coef, norm_gain, skip, gains):
    mag = jnp.exp(-rate)
    a_re, a_im = mag * jnp.cos(angle), mag * jnp.sin(angle)
    c1 = 2.0 * a_re
    c2 = -(mag * mag)
    b0 = 2.0 * coef[0]
    b1 = -2.0 * (coef[0] * a_re + coef[1] * a_im)
    return jnp.concatenate([c1, c2, b0, b1, norm_gain[None], skip[None], gains], axis=0)


def local(inputs, lengths, order, norm_gain, rate, angle, coef, skip, score_gains, out_proj):
    sections = lax.axis_size("pipe")
    seqs = lax.axis_size("seq")
    pipe = lax.axis_index("pipe")
    seq = lax.axis_index("seq")
    rows, width = inputs.shape[1], inputs.shape[2]
    modes = rate.shape[1]
    groups = width // LANES
    table = mode_table(rate[0], angle[0], coef[0], norm_gain[0], skip[0], score_gains[0]).reshape(-1, groups, LANES)
    vm = pl.BlockSpec(memory_space=pltpu.VMEM)
    sm = pl.BlockSpec(memory_space=pltpu.SMEM)
    hb = pl.BlockSpec(memory_space=pl.ANY)
    total = 2 * rows
    moves = 82
    whole, tabs, x = pl.pallas_call(
        functools.partial(comm_kernel, width, 896),
        out_shape=(jax.ShapeDtypeStruct((sections, YS, ZS, 2, out_proj.shape[1], width), jnp.bfloat16),
                   jax.ShapeDtypeStruct((sections,) + table.shape, jnp.float32),
                   jax.ShapeDtypeStruct((total, width), jnp.bfloat16)),
        in_specs=[sm, hb, hb, hb],
        out_specs=(hb, vm, vm),
        scratch_shapes=[
            pltpu.VMEM((sections, rows, width), jnp.bfloat16),
            pltpu.SemaphoreType.DMA((moves,)),
            pltpu.SemaphoreType.DMA((moves,)),
            pltpu.SemaphoreType.DMA((3,)),
        ],
        compiler_params=pltpu.CompilerParams(collective_id=0, has_side_effects=True, vmem_limit_bytes=32 << 20),
        name="exchange",
    )(order, out_proj[0], inputs[0], table)
    whole = whole.reshape(sections, width, width)

    chosen = lax.dynamic_index_in_dim(order, pipe, 0, False)
    positions = seq * rows - rows + jnp.arange(2 * rows)
    doc_ends = jnp.cumsum(lax.dynamic_index_in_dim(lengths, chosen, 0, False))
    counted = jnp.sum((doc_ends[None, :] <= positions[:, None]).astype(jnp.int32), axis=1)
    docs = jnp.where(positions >= 0, counted, -1)
    link = jnp.concatenate([jnp.zeros((1,), jnp.float32), (docs[1:] == docs[:-1]).astype(jnp.float32)])

    out = pl.pallas_call(
        functools.partial(compute_kernel, sections, modes, total, width),
        out_shape=jax.ShapeDtypeStruct((rows, width), jnp.bfloat16),
        in_specs=[vm, sm, vm, vm, vm, hb],
        out_specs=vm,
        scratch_shapes=[
            pltpu.VMEM((total, width), jnp.bfloat16),
            pltpu.VMEM((total * groups, LANES), jnp.float32),
            pltpu.VMEM((total * groups, LANES), jnp.float32),
            pltpu.VMEM((total, width), jnp.bfloat16),
            pltpu.VMEM((total, width), jnp.bfloat16),
            pltpu.VMEM((total, width), jnp.bfloat16),
            pltpu.VMEM((total, width), jnp.bfloat16),
            pltpu.VMEM((total, total), jnp.float32),
            pltpu.VMEM((2, width, width), jnp.bfloat16),
            pltpu.SemaphoreType.DMA((2,)),
        ],
        compiler_params=pltpu.CompilerParams(vmem_limit_bytes=56 << 20),
        name="sections",
    )(x, link[None], docs[:, None], docs[None, :], tabs, whole)
    return out[None]


def solution(mesh):
    in_specs = (
        P("pipe", "seq", None),
        P(),
        P(),
        P("pipe", None),
        P("pipe", None, None),
        P("pipe", None, None),
        P("pipe", None, None, None),
        P("pipe", None),
        P("pipe", None, None),
        P("pipe", "seq", None),
    )
    out_specs = P("pipe", "seq", None)
    return jax.shard_map(local, mesh=mesh, in_specs=in_specs, out_specs=out_specs, check_vma=False)
```

time: 1240 us -> 318 us (0.26); the launches traced: 1230 us -> 317 us
  other arithmetic: 580 us -> 4.07 us
  local copies, waits for them, and re-layouts: 354 us -> 9.79 us
  Pallas kernels: 0 us -> 302 us
  matrix products: 78.5 us -> 0 us
  starting transfers between devices: 76.1 us -> 0 us
  waiting for transfers between devices: 70.9 us -> 0 us
  between operations: 36.8 us -> 2.08 us
  blocking collectives: 28.1 us -> 0 us
    pallas_call x0 -> x2, Pallas kernels: none -> 302 us  [the longest x1 158 us: local(): pl.pallas_call(functools.partial(comm_kernel, width, 896), out_shape=(jax...]
    add x120 -> x1, other arithmetic: 295 us -> 0.01 us  [local(): positions = seq * rows - rows + jnp.arange(2 * rows)]
    dynamic_slice x113 -> x1, local copies, waits for them, and re-layouts: 129 us -> 1.24 us  [local(): chosen = lax.dynamic_index_in_dim(order, pipe, 0, False)]
    dynamic_update_slice x56 -> x0, local copies, waits for them, and re-layouts: 90.9 us -> none  [run_chain(): lax.scan(advance, (start_re, start_im), (local_re, local_im, link_flags))]
    reduce_sum x28 -> x0, other arithmetic: 86.9 us -> none  [the longest x7 53.8 us: finish_terms(): jnp.sum(carry_re[None] * enter_re[:, None] - carry_im[None] * enter_im[:,...]
    convert_element_type x82 -> x0, other arithmetic: 78.6 us -> none  [the longest x56 53.5 us: local_conv(): same_doc[:, :, None].astype(jnp.float32)]
    ppermute x20 -> x0, starting transfers between devices: 76.1 us -> none  [passed_along(): lax.ppermute(value, axis, [(source, source + steps) for source in range(i...]
    ppermute x20 -> x0, waiting for transfers between devices: 70.4 us -> none  [passed_along(): lax.ppermute(value, axis, [(source, source + steps) for source in range(i...]
  transfers between devices with their start and end apart: 22 -> 0, of which waited for: 12 -> 0; matrix products, arithmetic and copies ran while one was open for 28% -> 0% of each run, Pallas kernels for 0% -> 0%
where the time goes in v1:
time: 318 us; the launch traced here: 317 us
  Pallas kernels  302 us (95%)
  local copies, waits for them, and re-layouts  9.79 us (3%)
  other arithmetic  4.07 us (1%)
    pallas_call x1, Pallas kernels, local(): pl.pallas_call(functools.partial(comm_kernel, width, 896), out_shape=(jax...  158 us
    pallas_call x1, Pallas kernels, local(): pl.pallas_call(functools.partial(compute_kernel, sections, modes, total,...  144 us
    unnamed x24, local copies, waits for them, and re-layouts  7.51 us

profile of v1, /device:TPU:1, one launch (start us, length us, event | category | flops | bytes accessed | tf_op | source)
XLA Modules:
  0.0 317.5 jit_solution(4408692529665263341)
XLA Ops:
  0.0 0.0 copy-start
  0.0 1.5 multiply_bitcast_fusion
  1.5 1.0 slice_bitcast_fusion
  2.8 0.7 constant_dynamic-update-slice_fusion.1
  3.5 0.7 constant_dynamic-update-slice_fusion
  4.2 0.7 bitcast_dynamic-update-slice_fusion.tab_in
  4.9 0.0 copy-start.3
  4.9 1.0 copy-done.3
  5.9 0.0 copy-start.4
  5.9 0.9 copy-done.4
  6.8 0.0 copy-start.5
  6.8 0.7 copy-done.5
  7.5 158.0 %exchange.1 = (bf16[4,4,8,2,32,2048]{5,4,3,2,1,0:T(8,128)(2,1)}, f32[4,68,16,128]{3,2,1,0:T(8,128)S(1)}, bf16[256,2048]{1,0:T(8,128)(2,1)S(1)}) custom-call(s32[4]{0:T(128)S(1)} %copy-done.5, bf16[32,2048]{1,0:T(8,128)(2,1)S(1)} %bitcast.52, bf16[128,2048]{1,0:T(8,128)(2,1)S(1)} %bitcast.51, f32[68,16,128]{2,1,0:T(8,128)S(1)} %bitcast_dynamic-update-slice_fusion.tab_in), custom_call_target="tpu_custom_call" | custom-call | tf_op jit(solution)/shard_map/exchange/pallas_call | solution.py:307
  165.5 0.0 copy-start.1
  165.5 1.4 copy-done.1
  166.9 0.0 copy-start.2
  166.9 1.0 copy-done.2
  167.9 1.2 dynamic_slice.8
  171.0 0.0 copy-done
  171.1 0.3 reduce-window.9
  171.4 0.1 slice.24
  171.5 0.1 slice_reduce_fusion
  171.6 0.1 add_bitcast_fusion
  171.7 0.2 convert_reduce_fusion
  171.9 0.1 slice_compare_fusion
  171.9 0.6 add_convert_fusion
  172.6 0.1 copy.12
  172.7 0.7 fusion.2.docq_ref
  173.4 0.6 compare_select_fusion.dock_ref
  174.0 143.5 %sections.1 = bf16[128,2048]{1,0:T(8,128)(2,1)} custom-call(bf16[256,2048]{1,0:T(8,128)(2,1)} %copy-done.2, f32[1,256]{1,0:T(1,128)} %bitcast.60, s32[256,1]{1,0:T(8,128)} %fusion.2.docq_ref, s32[1,256]{1,0:T(1,128)} %compare_select_fusion.dock_ref, f32[4,68,16,128]{3,2,1,0:T(8,128)} %copy-done.1, bf16[4,2048,2048]{2,1,0:T(8,128)(2,1)} %bitcast.53), custom_call_target="tpu_custom_call" | custom-call | tf_op jit(solution)/shard_map/sections/pallas_call | solution.py:332
  (14 shorter events, 0.3 us)
Async XLA Ops:
  0.0 171.0 %copy-start = (s32[4,256]{1,0:T(4,128)S(1)}, s32[4,256]{1,0:T(4,128)}, u32[]{:S(2)}) copy-start(s32[4,256]{1,0:T(4,128)} %param.11) | copy-start | bytes 12292
  4.9 1.0 copy-start.3
  5.9 0.9 copy-start.4
  6.8 0.7 copy-start.5
  165.5 1.4 copy-start.1
  166.9 1.0 copy-start.2

commit v2 on v1

v2 whole, which is shorter than its diff:
```python
import functools

import jax
import jax.numpy as jnp
from jax import lax
from jax.experimental import pallas as pl
from jax.experimental.pallas import tpu as pltpu
from jax.sharding import PartitionSpec as P

HEAD_DIM = 128
LANES = 128
norm_eps = 1e-06
masked_score = -1e30


MESH = pl.DeviceIdType.MESH
ZS, YS, XS = 8, 4, 4


class Mover:
    def __init__(self, send_sems, recv_sems):
        self.send_sems, self.recv_sems, self.used, self.open = send_sems, recv_sems, 0, []

    def push(self, source, target, incoming, device):
        k = self.used
        self.used += 1
        out = pltpu.make_async_remote_copy(source, target, self.send_sems.at[k], self.recv_sems.at[k],
                                           device_id=device, device_id_type=MESH)
        out.start()
        back = pltpu.make_async_remote_copy(incoming, incoming, self.send_sems.at[k], self.recv_sems.at[k],
                                            device_id=device, device_id_type=MESH)
        self.open.append(out)
        return back.wait_recv

    def finish(self):
        for out in self.open:
            out.wait_send()
        self.open = []


def ring(mover, size, me, block, half, device, share=None):
    def at(shift):
        return lax.rem(me + (shift + size), size)
    waits = {}

    def step(t):
        def go():
            if t > 1:
                waits[t - 1, 0]()
                waits[t - 1, 1]()
            if t <= size // 2:
                pick = (lambda i, k: half(i, k)) if t == size // 2 else (lambda i, k: block(i))
                ahead, behind = at(1 - t), at(t - 1)
                waits[t, 0] = mover.push(pick(ahead, 0), pick(ahead, 0), pick(at(-t), 0), device(at(1)))
                waits[t, 1] = mover.push(pick(behind, 1), pick(behind, 1), pick(at(t), 1), device(at(-1)))
            if share is not None:
                share(at(t - 1))
                if 1 < t <= size // 2:
                    share(at(1 - t))
        return go
    return [step(t) for t in range(1, size // 2 + 2)]


def transfer_steps(mover, refs, chosen, width, split):
    w_ref, in_ref, tab_in, wg, xin, tabs, x, local_sem = refs
    pipe, seq = lax.axis_index("pipe"), lax.axis_index("seq")
    core, z, y = lax.rem(seq, 2), lax.rem(seq // 2, ZS), seq // (2 * ZS)
    rows = in_ref.shape[0]
    nseq = 2 * ZS * YS

    def seq_of(yy, zz, cc):
        return (yy * ZS + zz) * 2 + cc

    def to_x(i):
        return (i, seq)

    def to_y(i):
        return (pipe, seq_of(i, z, core))

    def to_z(i):
        return (pipe, seq_of(y, i, core))

    partner = (pipe, seq_of(y, z, 1 - core))
    following = (pipe, lax.rem(seq + 1, nseq))
    preceding = (pipe, lax.rem(seq + nseq - 1, nseq))
    peers = [to_x(lax.rem(pipe + 1, XS)), to_x(lax.rem(pipe + 3, XS)), to_y(lax.rem(y + 1, YS)), to_y(lax.rem(y + 3, YS)),
             to_z(lax.rem(z + 1, ZS)), to_z(lax.rem(z + 7, ZS)), partner, following, preceding]
    trows = tabs.shape[1] // 2
    tlow = pl.ds(core * trows, trows)
    tpart = [pl.ds(core * trows + k * (trows // 2), trows // 2) for k in range(2)]
    depth = w_ref.shape[0]

    def begin():
        bar = pltpu.get_barrier_semaphore()
        for peer in peers:
            pl.semaphore_signal(bar, inc=1, device_id=peer, device_id_type=MESH)
        pl.semaphore_wait(bar, len(peers))
        copies = [pltpu.make_async_copy(w_ref, wg.at[pipe, y, z, core], local_sem.at[0]),
                  pltpu.make_async_copy(in_ref, xin.at[pipe], local_sem.at[1]),
                  pltpu.make_async_copy(tab_in.at[tlow], tabs.at[pipe, tlow], local_sem.at[2])]
        for c in copies:
            c.start()
        for c in copies:
            c.wait()

    xw = ring(mover, XS, pipe, lambda i: wg.at[i, y, z, core],
              lambda i, k: wg.at[i, y, z, core, pl.ds(k * (depth // 2), depth // 2)], to_x)
    xi = ring(mover, XS, pipe, lambda i: xin.at[i], lambda i, k: xin.at[i, pl.ds(k * (rows // 2), rows // 2)], to_x)
    xt = ring(mover, XS, pipe, lambda i: tabs.at[i, tlow], lambda i, k: tabs.at[i, tpart[k]], to_x)
    ca, cb = pl.ds(0, split), pl.ds(split, width - split)
    pair = [pl.ds(0, XS // 2), pl.ds(XS // 2, XS // 2)]
    ya = ring(mover, YS, y, lambda i: wg.at[:, i, z, core, :, ca], lambda i, k: wg.at[pair[k], i, z, core, :, ca], to_y)
    zb = ring(mover, ZS, z, lambda i: wg.at[:, y, i, core, :, cb], lambda i, k: wg.at[pair[k], y, i, core, :, cb], to_z)
    held = {}

    def choose():
        x[pl.ds(rows, rows), :] = xin[chosen]
        held["halo"] = mover.push(x.at[pl.ds(rows, rows)], x.at[pl.ds(0, rows)], x.at[pl.ds(0, rows)], following)

    def share_tables():
        other = pl.ds((1 - core) * trows, trows)
        held["tabs"] = mover.push(tabs.at[:, tlow], tabs.at[:, tlow], tabs.at[:, other], partner)

    shared = {s: [] for s in range(XS)}

    def last(s):
        yh = [pl.ds(0, YS // 2), pl.ds(YS // 2, YS // 2)]
        zh = [pl.ds(0, ZS // 2), pl.ds(ZS // 2, ZS // 2)]

        def to_partner(part):
            def share(i):
                shared[s].append(mover.push(part(i, core), part(i, core), part(i, 1 - core), partner))
            return share
        part_a = lambda i, c: wg.at[s, :, i, c, :, ca]
        part_b = lambda i, c: wg.at[s, i, :, c, :, cb]
        za = ring(mover, ZS, z, lambda i: part_a(i, core), lambda i, k: wg.at[s, yh[k], i, core, :, ca], to_z, to_partner(part_a))
        yb = ring(mover, YS, y, lambda i: part_b(i, core), lambda i, k: wg.at[s, i, zh[k], core, :, cb], to_y, to_partner(part_b))
        return za, yb

    finals = [last(s) for s in range(XS)]
    early = [begin, xw[0], xw[1], xi[0], xw[2], ya[0], zb[0], xt[0], zb[1], ya[1], xi[1], zb[2], ya[2], zb[3], xt[1], xi[2], choose,
             xt[2], share_tables, zb[4], finals[0][1][0], finals[0][0][0]]
    per_section = []
    for s in range(XS):
        za, yb = finals[s]
        steps = [za[1], za[2], yb[1], za[3]]
        if s + 1 < XS:
            steps += [lambda s=s: (finals[s + 1][1][0](), finals[s + 1][0][0]())]
        steps += [za[4], yb[2]]
        per_section.append(steps)

    def arrived(s):
        for wait in shared[s]:
            wait()
    return early, held, per_section, arrived


def document_masks(lengths_ref, chosen, first, rows, bias, links):
    f32, bf16 = jnp.float32, jnp.bfloat16
    count = lengths_ref.shape[1]
    own = rows // 2
    sizes = jnp.broadcast_to(lengths_ref[pl.ds(chosen, 1), :].astype(f32), (8, count)).astype(bf16)
    low = (lax.broadcasted_iota(jnp.int32, (count, count), 1) <= lax.broadcasted_iota(jnp.int32, (count, count), 0))
    low = low.astype(f32).astype(bf16)
    both = (((1,), (1,)), ((), ()))
    ends_row = lax.dot_general(sizes, low, both, preferred_element_type=f32)[0:1, :].astype(jnp.int32)
    ends_col = lax.dot_general(low, sizes, both, preferred_element_type=f32)[:, 0:1].astype(jnp.int32)
    index = lax.broadcasted_iota(jnp.int32, (rows, count), 0)
    down = index + first

    def doc_col(pos):
        counted = jnp.sum(jnp.where(ends_row <= pos, 1.0, 0.0), axis=1, keepdims=True)
        return jnp.where(pos[:, 0:1] >= 0, counted, -1.0)
    docs = doc_col(down)
    before = doc_col(down - 1)
    across = lax.broadcasted_iota(jnp.int32, (count, rows), 1) + first
    docs_row = jnp.sum(jnp.where(ends_col <= across, 1.0, 0.0), axis=0, keepdims=True)
    docs_row = jnp.where(across[0:1, :] >= 0, docs_row, -1.0)
    good = (docs == docs_row) & (lax.broadcasted_iota(jnp.int32, (rows, rows), 1) <= lax.broadcasted_iota(jnp.int32, (rows, rows), 0))
    bias[...] = jnp.where(good, 0.0, masked_score)
    link = jnp.where((docs == before) & (index[:, 0:1] > 0), 1.0, 0.0)
    wide = jnp.broadcast_to(link, (rows, LANES))
    for r in range(rows // 8):
        for j in range(8):
            links[pl.ds(r * 64 + j, 8, stride=8), :] = wide[r * 8:r * 8 + 8]


def fused_kernel(width, split, modes, order_ref, lengths_ref, w_ref, in_ref, tab_in, o_ref,
                 wg, tab_ref, cur, xin, xs, ys, mid, qs, ks, att, bias, links, send_sems, recv_sems, local_sem):
    sections = wg.shape[0]
    rows = cur.shape[0]
    groups = width // LANES
    halves = groups // 8
    own = rows // 2
    f32, bf16 = jnp.float32, jnp.bfloat16
    mover = Mover(send_sems, recv_sems)
    chosen = order_ref[lax.axis_index("pipe")]
    early, held, per_section, arrived = transfer_steps(
        mover, (w_ref, in_ref, tab_in, wg, xin, tab_ref, cur, local_sem), chosen, width, split)
    for k, step in enumerate(early):
        step()
        if k == 3:
            document_masks(lengths_ref, chosen, (lax.axis_index("seq") - 1) * own, rows, bias, links)
    held["halo"]()
    held["tabs"]()
    queue = []

    def serve(n=1):
        for _ in range(min(n, len(queue))):
            queue.pop(0)()

    for s in range(sections):
        queue += per_section[s]

        def spread(r, c, s=s):
            base = pl.multiple_of(r * 16, 16)
            xb = cur[pl.ds(base, 16), :].astype(f32)
            inv = lax.rsqrt(jnp.mean(xb * xb, axis=1, keepdims=True) + norm_eps)
            for g in range(groups):
                sc = xb[:, g * LANES:(g + 1) * LANES] * inv * tab_ref[s, 4 * modes, g:g + 1, :]
                for h in range(2):
                    xs[pl.ds((base + 8 * h) * groups + g, 8, stride=groups), :] = sc[8 * h:8 * h + 8]
            return c

        lax.fori_loop(0, rows // 16, spread, 0)
        serve()

        per = 8
        for hf in range(halves):
            for mg in range(modes // per):
                part = slice(8 * hf, 8 * hf + 8)
                c1 = [tab_ref[s, mg * per + m, part, :] for m in range(per)]
                c2 = [tab_ref[s, modes + mg * per + m, part, :] for m in range(per)]
                b0 = [tab_ref[s, 2 * modes + mg * per + m, part, :] for m in range(per)]
                b1 = [tab_ref[s, 3 * modes + mg * per + m, part, :] for m in range(per)]
                skip = tab_ref[s, 4 * modes + 1, part, :]

                def step(p0, state, c1=c1, c2=c2, b0=b0, b1=b1, skip=skip, hf=hf, mg=mg):
                    w1, w2 = list(state[:per]), list(state[per:])
                    for u in range(4):
                        p = p0 * 4 + u
                        at = pl.multiple_of(p * groups + 8 * hf, 8)
                        x = xs[pl.ds(at, 8), :]
                        link = links[pl.ds(pl.multiple_of(p * 8, 8), 8), :]
                        acc = skip * x if mg == 0 else ys[pl.ds(at, 8), :]
                        parts = []
                        for m in range(per):
                            k1 = w1[m] * link
                            k2 = w2[m] * link
                            w = x + (c1[m] * k1 + c2[m] * k2)
                            parts.append(b0[m] * w + b1[m] * k1)
                            w1[m], w2[m] = w, k1
                        while len(parts) > 1:
                            parts = [parts[i] + parts[i + 1] for i in range(0, len(parts), 2)]
                        ys[pl.ds(at, 8), :] = acc + parts[0]
                    return tuple(w1) + tuple(w2)

                zero = jnp.zeros((8, LANES), f32)
                lax.fori_loop(0, rows // 4, step, (zero,) * (2 * per))
                serve()

        def gather(r, c, s=s):
            base = pl.multiple_of(r * 16, 16)
            sq = jnp.zeros((16, LANES), f32)
            for g in range(groups):
                lanes = slice(g * LANES, (g + 1) * LANES)
                mixed = jnp.concatenate(
                    [ys[pl.ds((base + 8 * h) * groups + g, 8, stride=groups), :] for h in range(2)], axis=0)
                mb = (cur[pl.ds(base, 16), lanes].astype(f32) + mixed).astype(bf16)
                mid[pl.ds(base, 16), lanes] = mb
                mf = mb.astype(f32)
                sq = sq + mf * mf
            inv = lax.rsqrt(jnp.sum(sq, axis=1, keepdims=True) * (1.0 / width) + norm_eps)
            for g in range(groups):
                lanes = slice(g * LANES, (g + 1) * LANES)
                normed = mid[pl.ds(base, 16), lanes].astype(f32) * inv
                qs[pl.ds(base, 16), lanes] = (normed * tab_ref[s, 4 * modes + 2, g:g + 1, :]).astype(bf16)
                ks[pl.ds(base, 16), lanes] = (normed * tab_ref[s, 4 * modes + 3, g:g + 1, :]).astype(bf16)
            return c

        lax.fori_loop(0, rows // 16, gather, 0)
        serve()

        final = s == sections - 1
        together = 4
        scale = HEAD_DIM ** (-0.5) * 1.4426950408889634

        def heads(i, c, final=final):
            work = []
            for j in range(together):
                lanes = pl.ds(pl.multiple_of((i * together + j) * HEAD_DIM, HEAD_DIM), HEAD_DIM)
                for half in ((1,) if final else (0, 1)):
                    work.append((lanes, slice(half * own, (half + 1) * own), slice(0, (half + 1) * own)))
            scores = [lax.dot_general(qs[q, lanes], ks[k, lanes], (((1,), (1,)), ((), ())), preferred_element_type=f32)
                      * scale + bias[q, k] for lanes, q, k in work]
            raw = [jnp.exp2(sc - jnp.max(sc, axis=1, keepdims=True)) for sc in scores]
            weights = [(e * (1.0 / jnp.sum(e, axis=1, keepdims=True))).astype(bf16) for e in raw]
            for (lanes, q, k), wt in zip(work, weights):
                att[q, lanes] = jnp.dot(wt, mid[k, lanes], preferred_element_type=f32).astype(bf16)
            return c

        steps = width // HEAD_DIM // together
        lax.fori_loop(0, steps // 2, heads, 0)
        serve()
        lax.fori_loop(steps // 2, steps, heads, 0)
        serve(len(queue))
        arrived(s)
        if s == 0:
            mover.finish()
        cols = 256

        def project(n, c, s=s, final=final):
            lanes = pl.ds(pl.multiple_of(n * cols, cols), cols)
            r = slice(own, rows) if final else slice(0, rows)
            weight = wg[s, :, :, :, :, lanes].reshape(width, cols)
            acc = jnp.dot(att[r, :], weight, preferred_element_type=f32)
            result = (mid[r, lanes].astype(f32) + acc).astype(bf16)
            if final:
                o_ref[:, lanes] = result
            else:
                cur[:, lanes] = result
            return c

        lax.fori_loop(0, width // cols, project, 0)
    mover.finish()


def mode_table(rate, angle, coef, norm_gain, skip, gains):
    mag = jnp.exp(-rate)
    a_re, a_im = mag * jnp.cos(angle), mag * jnp.sin(angle)
    c1 = 2.0 * a_re
    c2 = -(mag * mag)
    b0 = 2.0 * coef[0]
    b1 = -2.0 * (coef[0] * a_re + coef[1] * a_im)
    return jnp.concatenate([c1, c2, b0, b1, norm_gain[None], skip[None], gains], axis=0)


def local(inputs, lengths, order, norm_gain, rate, angle, coef, skip, score_gains, out_proj):
    sections = lax.axis_size("pipe")
    rows, width = inputs.shape[1], inputs.shape[2]
    modes = rate.shape[1]
    groups = width // LANES
    table = mode_table(rate[0], angle[0], coef[0], norm_gain[0], skip[0], score_gains[0]).reshape(-1, groups, LANES)
    vm = pl.BlockSpec(memory_space=pltpu.VMEM)
    sm = pl.BlockSpec(memory_space=pltpu.SMEM)
    hb = pl.BlockSpec(memory_space=pl.ANY)
    total = 2 * rows
    moves = 128
    depth = out_proj.shape[1]
    wide = lambda: pltpu.VMEM((total, width), jnp.bfloat16)
    tall = lambda: pltpu.VMEM((total * groups, LANES), jnp.float32)
    out = pl.pallas_call(
        functools.partial(fused_kernel, width, 896, modes),
        out_shape=jax.ShapeDtypeStruct((rows, width), jnp.bfloat16),
        in_specs=[sm, vm, hb, hb, hb],
        out_specs=vm,
        scratch_shapes=[
            pltpu.VMEM((sections, YS, ZS, 2, depth, width), jnp.bfloat16),
            pltpu.VMEM((sections,) + table.shape, jnp.float32),
            wide(),
            pltpu.VMEM((sections, rows, width), jnp.bfloat16),
            tall(), tall(), wide(), wide(), wide(), wide(),
            pltpu.VMEM((total, total), jnp.float32),
            pltpu.VMEM((total * 8, LANES), jnp.float32),
            pltpu.SemaphoreType.DMA((moves,)),
            pltpu.SemaphoreType.DMA((moves,)),
            pltpu.SemaphoreType.DMA((3,)),
        ],
        compiler_params=pltpu.CompilerParams(collective_id=0, has_side_effects=True, vmem_limit_bytes=58 << 20),
        name="sections",
    )(order, lengths, out_proj[0], inputs[0], table)
    return out[None]


def solution(mesh):
    in_specs = (
        P("pipe", "seq", None),
        P(),
        P(),
        P("pipe", None),
        P("pipe", None, None),
        P("pipe", None, None),
        P("pipe", None, None, None),
        P("pipe", None),
        P("pipe", None, None),
        P("pipe", "seq", None),
    )
    out_specs = P("pipe", "seq", None)
    return jax.shard_map(local, mesh=mesh, in_specs=in_specs, out_specs=out_specs, check_vma=False)
```

time: 318 us -> 192 us (0.60)
  Pallas kernels: 302 us -> 185 us
  local copies, waits for them, and re-layouts: 9.79 us -> 6.16 us
  other arithmetic: 4.07 us -> 0.53 us
    pallas_call x2 -> x1, Pallas kernels: 302 us -> 185 us  [local(): pl.pallas_call(functools.partial(fused_kernel, width, 896, modes), out_sh...]
    unnamed x24 -> x25, local copies, waits for them, and re-layouts: 7.51 us -> 6.16 us
where the time goes in v2:
time: 192 us
  Pallas kernels  185 us (96%)
  local copies, waits for them, and re-layouts  6.16 us (3%)
    pallas_call x1, Pallas kernels, local(): pl.pallas_call(functools.partial(fused_kernel, width, 896, modes), out_sh...  185 us
    unnamed x25, local copies, waits for them, and re-layouts  6.16 us

profile of v2, /device:TPU:1, one launch (start us, length us, event | category | flops | bytes accessed | tf_op | source)
XLA Modules:
  0.0 191.8 jit_solution(1250585187776068603)
XLA Ops:
  0.0 1.0 slice_bitcast_fusion
  1.0 0.0 copy-start.1
  1.0 0.0 copy-start.2
  1.1 0.8 copy-done.1
  1.9 0.1 copy-done.2
  2.0 0.5 multiply_bitcast_fusion
  2.7 0.0 copy-start.4
  2.7 0.0 copy-start.5
  2.7 0.7 copy-done.4
  3.4 0.0 copy-start.3
  3.4 0.0 copy-done.5
  3.4 0.7 copy-done.3
  4.1 0.0 copy-start
  4.1 0.8 copy-done
  4.9 185.0 %sections.1 = bf16[128,2048]{1,0:T(8,128)(2,1)} custom-call(s32[4]{0:T(128)} %order_ref.1, s32[4,256]{1,0:T(4,128)} %lengths_ref.1, bf16[32,2048]{1,0:T(8,128)(2,1)} %bitcast.46, bf16[128,2048]{1,0:T(8,128)(2,1)} %bitcast.44, f32[68,16,128]{2,1,0:T(8,128)} %copy-done), custom_call_target="tpu_custom_call" | custom-call | tf_op jit(solution)/shard_map/sections/pallas_call | solution.py:352
  190.0 1.9 copy.25
  (13 shorter events, 0.2 us)
Async XLA Ops:
  1.0 0.9 copy-start.1
  1.0 1.0 copy-start.2
  2.7 0.7 copy-start.4
  2.7 0.7 copy-start.5
  3.4 0.7 copy-start.3
  4.1 0.8 copy-start

commit v3 on v2

--- a/solution.py
+++ b/solution.py
@@ -108,14 +108,12 @@
     xi = ring(mover, XS, pipe, lambda i: xin.at[i], lambda i, k: xin.at[i, pl.ds(k * (rows // 2), rows // 2)], to_x)
     xt = ring(mover, XS, pipe, lambda i: tabs.at[i, tlow], lambda i, k: tabs.at[i, tpart[k]], to_x)
     ca, cb = pl.ds(0, split), pl.ds(split, width - split)
-    pair = [pl.ds(0, XS // 2), pl.ds(XS // 2, XS // 2)]
-    ya = ring(mover, YS, y, lambda i: wg.at[:, i, z, core, :, ca], lambda i, k: wg.at[pair[k], i, z, core, :, ca], to_y)
-    zb = ring(mover, ZS, z, lambda i: wg.at[:, y, i, core, :, cb], lambda i, k: wg.at[pair[k], y, i, core, :, cb], to_z)
     held = {}
 
     def choose():
         x[pl.ds(rows, rows), :] = xin[chosen]
         held["halo"] = mover.push(x.at[pl.ds(rows, rows)], x.at[pl.ds(0, rows)], x.at[pl.ds(0, rows)], following)
+        held["sent"] = mover.open.pop().wait_send
 
     def share_tables():
         other = pl.ds((1 - core) * trows, trows)
@@ -137,22 +135,40 @@
         yb = ring(mover, YS, y, lambda i: part_b(i, core), lambda i, k: wg.at[s, i, zh[k], core, :, cb], to_y, to_partner(part_b))
         return za, yb
 
+    def first(s):
+        ya = ring(mover, YS, y, lambda i: wg.at[s, i, z, core, :, ca],
+                  lambda i, k: wg.at[s, i, z, core, pl.ds(k * (depth // 2), depth // 2), ca], to_y)
+        zb = ring(mover, ZS, z, lambda i: wg.at[s, y, i, core, :, cb],
+                  lambda i, k: wg.at[s, y, i, core, pl.ds(k * (depth // 2), depth // 2), cb], to_z)
+        return zb, ya
+
+    firsts = [first(s) for s in range(XS)]
     finals = [last(s) for s in range(XS)]
-    early = [begin, xw[0], xw[1], xi[0], xw[2], ya[0], zb[0], xt[0], zb[1], ya[1], xi[1], zb[2], ya[2], zb[3], xt[1], xi[2], choose,
-             xt[2], share_tables, zb[4], finals[0][1][0], finals[0][0][0]]
-    per_section = []
-    for s in range(XS):
-        za, yb = finals[s]
-        steps = [za[1], za[2], yb[1], za[3]]
-        if s + 1 < XS:
-            steps += [lambda s=s: (finals[s + 1][1][0](), finals[s + 1][0][0]())]
-        steps += [za[4], yb[2]]
-        per_section.append(steps)
+
+    def advance(long_short, k):
+        long_short[0][k - 1]()
+        if k % 2:
+            long_short[1][k // 2]()
+
+    def tick(s, k):
+        def go():
+            advance(finals[s], k)
+            if s + 1 < XS:
+                advance(firsts[s + 1], k)
+            if k == 5 and s + 1 < XS:
+                tick(s + 1, 1)()
+        return go
+
+    def prepare(k):
+        return lambda: advance(firsts[0], k)
+    early = [begin, xw[0], xi[0], xw[1], xw[2], prepare(1), prepare(2), prepare(3), xi[1], xt[0], prepare(4), prepare(5),
+             tick(0, 1), xi[2], choose, xt[1], tick(0, 2), xt[2], share_tables]
+    ticks = [(s, tick(s, k)) for s in range(XS) for k in range(2, 6)][1:]
 
     def arrived(s):
         for wait in shared[s]:
             wait()
-    return early, held, per_section, arrived
+    return early, held, ticks, arrived
 
 
 def document_masks(lengths_ref, chosen, first, rows, bias, links):
@@ -195,7 +211,7 @@
     f32, bf16 = jnp.float32, jnp.bfloat16
     mover = Mover(send_sems, recv_sems)
     chosen = order_ref[lax.axis_index("pipe")]
-    early, held, per_section, arrived = transfer_steps(
+    early, held, queue, arrived = transfer_steps(
         mover, (w_ref, in_ref, tab_in, wg, xin, tab_ref, cur, local_sem), chosen, width, split)
     for k, step in enumerate(early):
         step()
@@ -203,15 +219,12 @@
             document_masks(lengths_ref, chosen, (lax.axis_index("seq") - 1) * own, rows, bias, links)
     held["halo"]()
     held["tabs"]()
-    queue = []
-
-    def serve(n=1):
-        for _ in range(min(n, len(queue))):
-            queue.pop(0)()
+
+    def serve():
+        if queue:
+            queue.pop(0)[1]()
 
     for s in range(sections):
-        queue += per_section[s]
-
         def spread(r, c, s=s):
             base = pl.multiple_of(r * 16, 16)
             xb = cur[pl.ds(base, 16), :].astype(f32)
@@ -223,7 +236,6 @@
             return c
 
         lax.fori_loop(0, rows // 16, spread, 0)
-        serve()
 
         per = 8
         for hf in range(halves):
@@ -243,21 +255,21 @@
                         x = xs[pl.ds(at, 8), :]
                         link = links[pl.ds(pl.multiple_of(p * 8, 8), 8), :]
                         acc = skip * x if mg == 0 else ys[pl.ds(at, 8), :]
-                        parts = []
+                        side = None
                         for m in range(per):
                             k1 = w1[m] * link
                             k2 = w2[m] * link
                             w = x + (c1[m] * k1 + c2[m] * k2)
-                            parts.append(b0[m] * w + b1[m] * k1)
+                            acc = acc + b0[m] * w
+                            side = b1[m] * k1 if side is None else side + b1[m] * k1
                             w1[m], w2[m] = w, k1
-                        while len(parts) > 1:
-                            parts = [parts[i] + parts[i + 1] for i in range(0, len(parts), 2)]
-                        ys[pl.ds(at, 8), :] = acc + parts[0]
+                        ys[pl.ds(at, 8), :] = acc + side
                     return tuple(w1) + tuple(w2)
 
                 zero = jnp.zeros((8, LANES), f32)
                 lax.fori_loop(0, rows // 4, step, (zero,) * (2 * per))
-                serve()
+                if mg == 0:
+                    serve()
 
         def gather(r, c, s=s):
             base = pl.multiple_of(r * 16, 16)
@@ -299,14 +311,13 @@
                 att[q, lanes] = jnp.dot(wt, mid[k, lanes], preferred_element_type=f32).astype(bf16)
             return c
 
-        steps = width // HEAD_DIM // together
-        lax.fori_loop(0, steps // 2, heads, 0)
+        lax.fori_loop(0, width // HEAD_DIM // together, heads, 0)
         serve()
-        lax.fori_loop(steps // 2, steps, heads, 0)
-        serve(len(queue))
+        while queue and queue[0][0] <= s:
+            serve()
         arrived(s)
         if s == 0:
-            mover.finish()
+            held["sent"]()
         cols = 256
 
         def project(n, c, s=s, final=final):
@@ -345,12 +356,12 @@
     sm = pl.BlockSpec(memory_space=pltpu.SMEM)
     hb = pl.BlockSpec(memory_space=pl.ANY)
     total = 2 * rows
-    moves = 128
+    moves = 160
     depth = out_proj.shape[1]
     wide = lambda: pltpu.VMEM((total, width), jnp.bfloat16)
     tall = lambda: pltpu.VMEM((total * groups, LANES), jnp.float32)
     out = pl.pallas_call(
-        functools.partial(fused_kernel, width, 896, modes),
+        functools.partial(fused_kernel, width, 768, modes),
         out_shape=jax.ShapeDtypeStruct((rows, width), jnp.bfloat16),
         in_specs=[sm, vm, hb, hb, hb],
         out_specs=vm,

time: 192 us -> 182 us (0.948)
  Pallas kernels: 185 us -> 175 us
    pallas_call x1, Pallas kernels: 185 us -> 175 us  [local(): pl.pallas_call(functools.partial(fused_kernel, width, 768, modes), out_sh...]
where the time goes in v3:
time: 182 us
  Pallas kernels  175 us (96%)
  local copies, waits for them, and re-layouts  6.16 us (3%)
    pallas_call x1, Pallas kernels, local(): pl.pallas_call(functools.partial(fused_kernel, width, 768, modes), out_sh...  175 us
    unnamed x25, local copies, waits for them, and re-layouts  6.16 us

profile of v3, /device:TPU:1, one launch (start us, length us, event | category | flops | bytes accessed | tf_op | source)
XLA Modules:
  0.0 182.1 jit_solution(11107307268838992689)
XLA Ops:
  0.0 1.0 slice_bitcast_fusion
  1.0 0.0 copy-start.1
  1.0 0.0 copy-start.2
  1.1 0.8 copy-done.1
  1.9 0.1 copy-done.2
  2.0 0.5 multiply_bitcast_fusion
  2.7 0.0 copy-start.4
  2.7 0.0 copy-start.5
  2.7 0.7 copy-done.4
  3.4 0.0 copy-start.3
  3.4 0.0 copy-done.5
  3.4 0.7 copy-done.3
  4.1 0.0 copy-start
  4.1 0.8 copy-done
  4.9 175.3 %sections.1 = bf16[128,2048]{1,0:T(8,128)(2,1)} custom-call(s32[4]{0:T(128)} %order_ref.1, s32[4,256]{1,0:T(4,128)} %lengths_ref.1, bf16[32,2048]{1,0:T(8,128)(2,1)} %bitcast.46, bf16[128,2048]{1,0:T(8,128)(2,1)} %bitcast.44, f32[68,16,128]{2,1,0:T(8,128)} %copy-done), custom_call_target="tpu_custom_call" | custom-call | tf_op jit(solution)/shard_map/sections/pallas_call | solution.py:363
  180.3 1.9 %copy.25 = bf16[1,128,2048]{2,1,0:T(8,128)(2,1)} copy(bf16[1,128,2048]{2,1,0:T(8,128)(2,1)} %bitcast.43) | data formatting | bytes 1048576
  (13 shorter events, 0.2 us)
Async XLA Ops:
  1.0 0.9 copy-start.1
  1.0 1.0 copy-start.2
  2.7 0.7 copy-start.4
  2.7 0.7 copy-start.5
  3.4 0.7 copy-start.3
  4.1 0.8 copy-start
